TPU v7x, 512 devices: a whole 4x8x8 slice. The times are simulated.
512 devices in a mesh: samp: 32 (over x_hi, y, core), feat: 16 (over x_lo, z).
Axes of the slice: x: 4 (x_hi: 2, x_lo: 2; x = x_hi * 2 + x_lo), y: 8, z: 8, core: 2. Of those that a mesh axis runs over, the one named last changes fastest.
Arguments:
- labels: int32 [2097152], P('samp'), may hold values 0 or 1
- beta: float32 [1048576], P('feat'), may hold values from -1.2 to 1.2
- tile_rows: int32 [32, 16, 64], P('samp', 'feat'), may hold values from 0 to 511, as said below
- tile_cols: int32 [32, 16, 64], P('samp', 'feat'), may hold values from 0 to 511, as said below
- tile_values: bfloat16 [32, 16, 64, 128, 128], P('samp', 'feat'), may hold values from -0.5 to 0.5
- block_order: int32 [16, 16], P('feat'), may hold values from 0 to 511, as said below
- hess_inv: float32 [16, 16, 128, 128], P('feat')
Outputs:
- beta_new: float32 [1048576], P('feat')
- residual: float32 [2097152], P(('samp', 'feat'))
Inputs may be any that keep to these rules, and one draw needn't show every extreme that they name: `tile_rows`: row block numbers within a samp index. `tile_cols`: feature block numbers within a feat index. Each row of block_order holds 16 distinct block numbers.
All inputs are finite; a program needn't handle non-finite values. No bound on the sum of `labels` on one device may be relied on, other than what follows from the above.
Results may differ from a plain program's by a relative error of at most 0.0025.
Values sent between devices are 32-bit elements; how exact they have to be, the bound alone decides.
A program may use at most 64 MiB of HBM per device.

v0:
```python
import jax
import jax.numpy as jnp
from jax import lax
from jax.sharding import PartitionSpec as P

exact_prec = lax.Precision.HIGHEST
l1_penalty = 0.25


def from_behind(value, axis, steps):
    count = lax.axis_size(axis)
    pairs = [(source, (source + steps) % count) for source in range(count)]
    return lax.ppermute(value, axis, pairs)


def per_device(labels, beta, tile_rows, tile_cols, tile_values, block_order, hess_inv):
    cycle_size = lax.axis_size("feat")
    my_index = lax.axis_index("feat")
    row_ids = tile_rows[0, 0]
    col_ids = tile_cols[0, 0]
    values = tile_values[0, 0]
    tile_edge = values.shape[-1]
    row_blocks = labels.shape[0] // tile_edge
    group_blocks = row_blocks // cycle_size
    blocks = beta.reshape(-1, tile_edge)
    picked = jnp.take(blocks.astype(jnp.bfloat16), col_ids, axis=0)
    products = jnp.einsum("krc,kc->kr", values, picked, preferred_element_type=jnp.float32)
    placing = (row_ids[:, None] == jnp.arange(row_blocks, dtype=jnp.int32)[None, :]).astype(
        jnp.float32
    )
    partial_sum = jnp.dot(placing.T, products, precision=exact_prec)
    margins = lax.psum_scatter(partial_sum, "feat", scatter_dimension=0, tiled=True)
    probability = jax.nn.sigmoid(margins)
    weight = probability * (1.0 - probability)
    own_labels = lax.dynamic_slice_in_dim(
        labels.reshape(row_blocks, tile_edge), my_index * group_blocks, group_blocks, 0
    )
    residual = own_labels.astype(jnp.float32) - probability
    sub_ids = jnp.arange(group_blocks, dtype=jnp.int32)
    inverses = hess_inv[0]
    targets = block_order[0]

    def run_section(section_index, carry):
        blocks, residual, weight = carry
        group_index = (my_index - section_index) % cycle_size
        target = lax.dynamic_index_in_dim(targets, section_index, 0, keepdims=False)
        inverse = lax.dynamic_index_in_dim(inverses, section_index, 0, keepdims=False)
        offsets = row_ids - group_index * group_blocks
        matches = (col_ids == target) & (offsets >= 0) & (offsets < group_blocks)
        chosen = (offsets[:, None] == sub_ids[None, :]) & matches[:, None]
        rounded = residual.astype(jnp.bfloat16)
        resid_tiles = jnp.dot(
            chosen.astype(jnp.bfloat16), rounded, preferred_element_type=jnp.float32
        ).astype(jnp.bfloat16)
        local_grad = jnp.einsum(
            "krc,kr->c", values, resid_tiles, preferred_element_type=jnp.float32
        )
        gradient = lax.psum(local_grad, "samp")
        current = lax.dynamic_index_in_dim(blocks, target, 0, keepdims=False)
        moved_block = current + jnp.dot(inverse, gradient, precision=exact_prec)
        shrunk = jnp.sign(moved_block) * jnp.maximum(jnp.abs(moved_block) - l1_penalty, 0.0)
        change = (shrunk - current).astype(jnp.bfloat16)
        image_rows = jnp.einsum("krc,c->kr", values, change, preferred_element_type=jnp.float32)
        landed = jnp.dot(chosen.astype(jnp.float32).T, image_rows, precision=exact_prec)
        residual = residual - weight * landed
        blocks = lax.dynamic_update_index_in_dim(blocks, shrunk, target, 0)
        residual, weight = from_behind((residual, weight), "feat", 1)
        return (blocks, residual, weight)

    blocks, residual, weight = lax.fori_loop(0, cycle_size, run_section, (blocks, residual, weight))
    return (blocks.reshape(-1), residual.reshape(-1))


def solution(mesh):
    placed = (
        P("samp"),
        P("feat"),
        P("samp", "feat", None),
        P("samp", "feat", None),
        P("samp", "feat", None, None, None),
        P("feat", None),
        P("feat", None, None, None),
    )
    return jax.shard_map(
        per_device,
        mesh=mesh,
        in_specs=placed,
        out_specs=(P("feat"), P(("samp", "feat"))),
        check_vma=False,
    )
```

profile of v0, /device:TPU:1, one launch (start us, length us, event | category | flops | bytes accessed | tf_op | source)
XLA Modules:
  0.0 1390.1 jit_solution(13827757922583052736)
XLA Ops:
  10.4 2.8 fusion.28
  14.4 68.1 %reduce-scatter.2.cloned.1.call-done = f32[32,128]{1,0:T(8,128)} async-done(((f32[512,128]{1,0:T(8,128)}), f32[32,128]{1,0:T(8,128)}) %reduce-scatter.2.cloned.1.call-update) | async-done | bytes 16400 | tf_op jit(solution)/shard_map/reduce_scatter | solution.py:32
  83.2 1299.3 %while.20 = (s32[]{:T(128)}, f32[512,128]{1,0:T(8,128)S(1)}, f32[32,128]{1,0:T(8,128)S(1)}, f32[32,128]{1,0:T(8,128)S(1)}, s32[16]{0:T(128)S(1)}, /*index=5*/f32...) while((s32[]{:T(128)}, f32[512,128]{1,0:T(8,128)S(1)}, ...), condition=%wide.region_3.4_spmd.clone, body=%wide.region_1.3_spmd.clone.sunk | while | flops 8091154 | bytes 4595052 | solution.py:70
  83.3 1.9 collective-permute-start.1
  88.4 76.9 %psum.16 = f32[128]{0:T(128)S(1)} all-reduce(f32[128]{0:T(128)S(1)} %convolution_bitcast_fusion.3), channel_id=1, replica_groups=mesh['samp'=32,'feat'=16] {'samp'}, use_global_device_ids=true, to_apply=%region_2.2 | all-reduce | flops 128 | bytes 1024 | tf_op jit(solution)/shard_map/while/body/eval_jaxpr/psum | solution.py:58
  167.9 1.9 collective-permute-start
  169.9 4.9 collective-permute-done
  179.9 65.9 %psum.16 = f32[128]{0:T(128)S(1)} all-reduce(f32[128]{0:T(128)S(1)} %convolution_bitcast_fusion.3), channel_id=1, replica_groups=mesh['samp'=32,'feat'=16] {'samp'}, use_global_device_ids=true, to_apply=%region_2.2 | all-reduce | flops 128 | bytes 1024 | tf_op jit(solution)/shard_map/while/body/eval_jaxpr/psum | solution.py:58
  248.4 1.9 collective-permute-start
  250.4 4.9 collective-permute-done
  260.4 65.9 %psum.16 = f32[128]{0:T(128)S(1)} all-reduce(f32[128]{0:T(128)S(1)} %convolution_bitcast_fusion.3), channel_id=1, replica_groups=mesh['samp'=32,'feat'=16] {'samp'}, use_global_device_ids=true, to_apply=%region_2.2 | all-reduce | flops 128 | bytes 1024 | tf_op jit(solution)/shard_map/while/body/eval_jaxpr/psum | solution.py:58
  329.0 1.9 collective-permute-start
  330.9 4.9 collective-permute-done
  340.9 65.9 %psum.16 = f32[128]{0:T(128)S(1)} all-reduce(f32[128]{0:T(128)S(1)} %convolution_bitcast_fusion.3), channel_id=1, replica_groups=mesh['samp'=32,'feat'=16] {'samp'}, use_global_device_ids=true, to_apply=%region_2.2 | all-reduce | flops 128 | bytes 1024 | tf_op jit(solution)/shard_map/while/body/eval_jaxpr/psum | solution.py:58
  409.5 1.9 collective-permute-start
  411.4 4.9 collective-permute-done
  421.4 65.9 %psum.16 = f32[128]{0:T(128)S(1)} all-reduce(f32[128]{0:T(128)S(1)} %convolution_bitcast_fusion.3), channel_id=1, replica_groups=mesh['samp'=32,'feat'=16] {'samp'}, use_global_device_ids=true, to_apply=%region_2.2 | all-reduce | flops 128 | bytes 1024 | tf_op jit(solution)/shard_map/while/body/eval_jaxpr/psum | solution.py:58
  490.0 1.9 collective-permute-start
  492.0 4.9 collective-permute-done
  501.9 65.9 %psum.16 = f32[128]{0:T(128)S(1)} all-reduce(f32[128]{0:T(128)S(1)} %convolution_bitcast_fusion.3), channel_id=1, replica_groups=mesh['samp'=32,'feat'=16] {'samp'}, use_global_device_ids=true, to_apply=%region_2.2 | all-reduce | flops 128 | bytes 1024 | tf_op jit(solution)/shard_map/while/body/eval_jaxpr/psum | solution.py:58
  570.5 1.9 collective-permute-start
  572.5 4.9 collective-permute-done
  582.5 65.9 %psum.16 = f32[128]{0:T(128)S(1)} all-reduce(f32[128]{0:T(128)S(1)} %convolution_bitcast_fusion.3), channel_id=1, replica_groups=mesh['samp'=32,'feat'=16] {'samp'}, use_global_device_ids=true, to_apply=%region_2.2 | all-reduce | flops 128 | bytes 1024 | tf_op jit(solution)/shard_map/while/body/eval_jaxpr/psum | solution.py:58
  651.0 1.9 collective-permute-start
  653.0 4.9 collective-permute-done
  663.0 65.9 %psum.16 = f32[128]{0:T(128)S(1)} all-reduce(f32[128]{0:T(128)S(1)} %convolution_bitcast_fusion.3), channel_id=1, replica_groups=mesh['samp'=32,'feat'=16] {'samp'}, use_global_device_ids=true, to_apply=%region_2.2 | all-reduce | flops 128 | bytes 1024 | tf_op jit(solution)/shard_map/while/body/eval_jaxpr/psum | solution.py:58
  731.5 1.9 collective-permute-start
  733.5 4.9 collective-permute-done
  743.5 65.9 %psum.16 = f32[128]{0:T(128)S(1)} all-reduce(f32[128]{0:T(128)S(1)} %convolution_bitcast_fusion.3), channel_id=1, replica_groups=mesh['samp'=32,'feat'=16] {'samp'}, use_global_device_ids=true, to_apply=%region_2.2 | all-reduce | flops 128 | bytes 1024 | tf_op jit(solution)/shard_map/while/body/eval_jaxpr/psum | solution.py:58
  814.0 4.9 collective-permute-done
  824.0 65.9 %psum.16 = f32[128]{0:T(128)S(1)} all-reduce(f32[128]{0:T(128)S(1)} %convolution_bitcast_fusion.3), channel_id=1, replica_groups=mesh['samp'=32,'feat'=16] {'samp'}, use_global_device_ids=true, to_apply=%region_2.2 | all-reduce | flops 128 | bytes 1024 | tf_op jit(solution)/shard_map/while/body/eval_jaxpr/psum | solution.py:58
  892.6 1.9 collective-permute-start
  894.6 4.9 collective-permute-done
  904.5 65.9 %psum.16 = f32[128]{0:T(128)S(1)} all-reduce(f32[128]{0:T(128)S(1)} %convolution_bitcast_fusion.3), channel_id=1, replica_groups=mesh['samp'=32,'feat'=16] {'samp'}, use_global_device_ids=true, to_apply=%region_2.2 | all-reduce | flops 128 | bytes 1024 | tf_op jit(solution)/shard_map/while/body/eval_jaxpr/psum | solution.py:58
  975.1 4.9 collective-permute-done
  985.1 65.9 %psum.16 = f32[128]{0:T(128)S(1)} all-reduce(f32[128]{0:T(128)S(1)} %convolution_bitcast_fusion.3), channel_id=1, replica_groups=mesh['samp'=32,'feat'=16] {'samp'}, use_global_device_ids=true, to_apply=%region_2.2 | all-reduce | flops 128 | bytes 1024 | tf_op jit(solution)/shard_map/while/body/eval_jaxpr/psum | solution.py:58
  1053.6 1.9 collective-permute-start
  1055.6 4.9 collective-permute-done
  1065.6 65.9 %psum.16 = f32[128]{0:T(128)S(1)} all-reduce(f32[128]{0:T(128)S(1)} %convolution_bitcast_fusion.3), channel_id=1, replica_groups=mesh['samp'=32,'feat'=16] {'samp'}, use_global_device_ids=true, to_apply=%region_2.2 | all-reduce | flops 128 | bytes 1024 | tf_op jit(solution)/shard_map/while/body/eval_jaxpr/psum | solution.py:58
  1136.1 4.9 collective-permute-done
  1146.1 65.9 %psum.16 = f32[128]{0:T(128)S(1)} all-reduce(f32[128]{0:T(128)S(1)} %convolution_bitcast_fusion.3), channel_id=1, replica_groups=mesh['samp'=32,'feat'=16] {'samp'}, use_global_device_ids=true, to_apply=%region_2.2 | all-reduce | flops 128 | bytes 1024 | tf_op jit(solution)/shard_map/while/body/eval_jaxpr/psum | solution.py:58
  1214.7 1.9 collective-permute-start
  1216.6 4.9 collective-permute-done
  1226.6 65.9 %psum.16 = f32[128]{0:T(128)S(1)} all-reduce(f32[128]{0:T(128)S(1)} %convolution_bitcast_fusion.3), channel_id=1, replica_groups=mesh['samp'=32,'feat'=16] {'samp'}, use_global_device_ids=true, to_apply=%region_2.2 | all-reduce | flops 128 | bytes 1024 | tf_op jit(solution)/shard_map/while/body/eval_jaxpr/psum | solution.py:58
  1295.2 1.9 collective-permute-start
  1297.2 4.9 collective-permute-done
  1307.1 65.9 %psum.16 = f32[128]{0:T(128)S(1)} all-reduce(f32[128]{0:T(128)S(1)} %convolution_bitcast_fusion.3), channel_id=1, replica_groups=mesh['samp'=32,'feat'=16] {'samp'}, use_global_device_ids=true, to_apply=%region_2.2 | all-reduce | flops 128 | bytes 1024 | tf_op jit(solution)/shard_map/while/body/eval_jaxpr/psum | solution.py:58
  1377.7 4.9 collective-permute-done
  (201 shorter events, 104.3 us)
Async XLA Ops:
  7.2 6.0 copy-start.2
  7.2 76.0 %copy-start.3 = (s32[1,1,64]{2,1,0:T(1,128)S(1)}, s32[1,1,64]{2,1,0:T(1,128)}, u32[]{:S(2)}) copy-start(s32[1,1,64]{2,1,0:T(1,128)} %param.12) | copy-start | bytes 772
  7.2 76.0 %copy-start = (bf16[1,1,64,128,128]{4,3,2,1,0:T(8,128)(2,1)S(1)}, bf16[1,1,64,128,128]{4,3,2,1,0:T(8,128)(2,1)}, u32[]{:S(2)}) copy-start(bf16[1,1,64,128,128]{4,3,2,1,0:T(8,128)(2,1)} %param.13) | copy-start | bytes 6291460
  7.2 76.0 %copy-start.4 = (s32[1,16]{1,0:T(1,128)S(1)}, s32[1,16]{1,0:T(1,128)}, u32[]{:S(2)}) copy-start(s32[1,16]{1,0:T(1,128)} %param.14) | copy-start | bytes 196
  7.2 75.3 %reduce-scatter.2.cloned.1.call-start = ((), (), s32[]{:S(2)}) async-start(), calls=%async_computation.1 | async-start | bytes 278528 | tf_op jit(solution)/shard_map/reduce_scatter | solution.py:32
  83.3 86.6 %collective-permute-start.1 = (f32[32,128]{1,0:T(8,128)S(1)}, f32[32,128]{1,0:T(8,128)S(1)}, u32[]{:S(2)}, u32[]{:S(2)}) collective-permute-start(f32[32,128]{1,0:T(8,128)S(1)} %copy.27), channel_id=1, source_target_pairs={{0,1},{1,2},{2,3},{3,4},{4,5},{5,6},{6,7},{7,8},{8,9},{9,10},{10,1... | collective-permute-start | bytes 49160 | tf_op jit(solution)/shard_map/while/body/eval_jaxpr/ppermute | solution.py:13
  167.9 6.9 collective-permute-start
  174.8 75.6 %collective-permute-start.1 = (f32[32,128]{1,0:T(8,128)S(1)}, f32[32,128]{1,0:T(8,128)S(1)}, u32[]{:S(2)}, u32[]{:S(2)}) collective-permute-start(f32[32,128]{1,0:T(8,128)S(1)} %copy.27), channel_id=1, source_target_pairs={{0,1},{1,2},{2,3},{3,4},{4,5},{5,6},{6,7},{7,8},{8,9},{9,10},{10,1... | collective-permute-start | bytes 49160 | tf_op jit(solution)/shard_map/while/body/eval_jaxpr/ppermute | solution.py:13
  248.4 6.9 collective-permute-start
  255.3 75.6 %collective-permute-start.1 = (f32[32,128]{1,0:T(8,128)S(1)}, f32[32,128]{1,0:T(8,128)S(1)}, u32[]{:S(2)}, u32[]{:S(2)}) collective-permute-start(f32[32,128]{1,0:T(8,128)S(1)} %copy.27), channel_id=1, source_target_pairs={{0,1},{1,2},{2,3},{3,4},{4,5},{5,6},{6,7},{7,8},{8,9},{9,10},{10,1... | collective-permute-start | bytes 49160 | tf_op jit(solution)/shard_map/while/body/eval_jaxpr/ppermute | solution.py:13
  329.0 6.9 collective-permute-start
  335.8 75.6 %collective-permute-start.1 = (f32[32,128]{1,0:T(8,128)S(1)}, f32[32,128]{1,0:T(8,128)S(1)}, u32[]{:S(2)}, u32[]{:S(2)}) collective-permute-start(f32[32,128]{1,0:T(8,128)S(1)} %copy.27), channel_id=1, source_target_pairs={{0,1},{1,2},{2,3},{3,4},{4,5},{5,6},{6,7},{7,8},{8,9},{9,10},{10,1... | collective-permute-start | bytes 49160 | tf_op jit(solution)/shard_map/while/body/eval_jaxpr/ppermute | solution.py:13
  409.5 6.9 collective-permute-start
  416.3 75.6 %collective-permute-start.1 = (f32[32,128]{1,0:T(8,128)S(1)}, f32[32,128]{1,0:T(8,128)S(1)}, u32[]{:S(2)}, u32[]{:S(2)}) collective-permute-start(f32[32,128]{1,0:T(8,128)S(1)} %copy.27), channel_id=1, source_target_pairs={{0,1},{1,2},{2,3},{3,4},{4,5},{5,6},{6,7},{7,8},{8,9},{9,10},{10,1... | collective-permute-start | bytes 49160 | tf_op jit(solution)/shard_map/while/body/eval_jaxpr/ppermute | solution.py:13
  490.0 6.9 collective-permute-start
  496.9 75.6 %collective-permute-start.1 = (f32[32,128]{1,0:T(8,128)S(1)}, f32[32,128]{1,0:T(8,128)S(1)}, u32[]{:S(2)}, u32[]{:S(2)}) collective-permute-start(f32[32,128]{1,0:T(8,128)S(1)} %copy.27), channel_id=1, source_target_pairs={{0,1},{1,2},{2,3},{3,4},{4,5},{5,6},{6,7},{7,8},{8,9},{9,10},{10,1... | collective-permute-start | bytes 49160 | tf_op jit(solution)/shard_map/while/body/eval_jaxpr/ppermute | solution.py:13
  570.5 6.9 collective-permute-start
  577.4 75.6 %collective-permute-start.1 = (f32[32,128]{1,0:T(8,128)S(1)}, f32[32,128]{1,0:T(8,128)S(1)}, u32[]{:S(2)}, u32[]{:S(2)}) collective-permute-start(f32[32,128]{1,0:T(8,128)S(1)} %copy.27), channel_id=1, source_target_pairs={{0,1},{1,2},{2,3},{3,4},{4,5},{5,6},{6,7},{7,8},{8,9},{9,10},{10,1... | collective-permute-start | bytes 49160 | tf_op jit(solution)/shard_map/while/body/eval_jaxpr/ppermute | solution.py:13
  651.0 6.9 collective-permute-start
  657.9 75.6 %collective-permute-start.1 = (f32[32,128]{1,0:T(8,128)S(1)}, f32[32,128]{1,0:T(8,128)S(1)}, u32[]{:S(2)}, u32[]{:S(2)}) collective-permute-start(f32[32,128]{1,0:T(8,128)S(1)} %copy.27), channel_id=1, source_target_pairs={{0,1},{1,2},{2,3},{3,4},{4,5},{5,6},{6,7},{7,8},{8,9},{9,10},{10,1... | collective-permute-start | bytes 49160 | tf_op jit(solution)/shard_map/while/body/eval_jaxpr/ppermute | solution.py:13
  731.5 6.9 collective-permute-start
  738.4 75.6 %collective-permute-start.1 = (f32[32,128]{1,0:T(8,128)S(1)}, f32[32,128]{1,0:T(8,128)S(1)}, u32[]{:S(2)}, u32[]{:S(2)}) collective-permute-start(f32[32,128]{1,0:T(8,128)S(1)} %copy.27), channel_id=1, source_target_pairs={{0,1},{1,2},{2,3},{3,4},{4,5},{5,6},{6,7},{7,8},{8,9},{9,10},{10,1... | collective-permute-start | bytes 49160 | tf_op jit(solution)/shard_map/while/body/eval_jaxpr/ppermute | solution.py:13
  812.1 6.9 collective-permute-start
  818.9 75.6 %collective-permute-start.1 = (f32[32,128]{1,0:T(8,128)S(1)}, f32[32,128]{1,0:T(8,128)S(1)}, u32[]{:S(2)}, u32[]{:S(2)}) collective-permute-start(f32[32,128]{1,0:T(8,128)S(1)} %copy.27), channel_id=1, source_target_pairs={{0,1},{1,2},{2,3},{3,4},{4,5},{5,6},{6,7},{7,8},{8,9},{9,10},{10,1... | collective-permute-start | bytes 49160 | tf_op jit(solution)/shard_map/while/body/eval_jaxpr/ppermute | solution.py:13
  892.6 6.9 collective-permute-start
  899.5 75.6 %collective-permute-start.1 = (f32[32,128]{1,0:T(8,128)S(1)}, f32[32,128]{1,0:T(8,128)S(1)}, u32[]{:S(2)}, u32[]{:S(2)}) collective-permute-start(f32[32,128]{1,0:T(8,128)S(1)} %copy.27), channel_id=1, source_target_pairs={{0,1},{1,2},{2,3},{3,4},{4,5},{5,6},{6,7},{7,8},{8,9},{9,10},{10,1... | collective-permute-start | bytes 49160 | tf_op jit(solution)/shard_map/while/body/eval_jaxpr/ppermute | solution.py:13
  973.1 6.9 collective-permute-start
  980.0 75.6 %collective-permute-start.1 = (f32[32,128]{1,0:T(8,128)S(1)}, f32[32,128]{1,0:T(8,128)S(1)}, u32[]{:S(2)}, u32[]{:S(2)}) collective-permute-start(f32[32,128]{1,0:T(8,128)S(1)} %copy.27), channel_id=1, source_target_pairs={{0,1},{1,2},{2,3},{3,4},{4,5},{5,6},{6,7},{7,8},{8,9},{9,10},{10,1... | collective-permute-start | bytes 49160 | tf_op jit(solution)/shard_map/while/body/eval_jaxpr/ppermute | solution.py:13
  1053.6 6.9 collective-permute-start
  1060.5 75.6 %collective-permute-start.1 = (f32[32,128]{1,0:T(8,128)S(1)}, f32[32,128]{1,0:T(8,128)S(1)}, u32[]{:S(2)}, u32[]{:S(2)}) collective-permute-start(f32[32,128]{1,0:T(8,128)S(1)} %copy.27), channel_id=1, source_target_pairs={{0,1},{1,2},{2,3},{3,4},{4,5},{5,6},{6,7},{7,8},{8,9},{9,10},{10,1... | collective-permute-start | bytes 49160 | tf_op jit(solution)/shard_map/while/body/eval_jaxpr/ppermute | solution.py:13
  1134.1 6.9 collective-permute-start
  1141.0 75.6 %collective-permute-start.1 = (f32[32,128]{1,0:T(8,128)S(1)}, f32[32,128]{1,0:T(8,128)S(1)}, u32[]{:S(2)}, u32[]{:S(2)}) collective-permute-start(f32[32,128]{1,0:T(8,128)S(1)} %copy.27), channel_id=1, source_target_pairs={{0,1},{1,2},{2,3},{3,4},{4,5},{5,6},{6,7},{7,8},{8,9},{9,10},{10,1... | collective-permute-start | bytes 49160 | tf_op jit(solution)/shard_map/while/body/eval_jaxpr/ppermute | solution.py:13
  1214.7 6.9 collective-permute-start
  1221.5 75.6 %collective-permute-start.1 = (f32[32,128]{1,0:T(8,128)S(1)}, f32[32,128]{1,0:T(8,128)S(1)}, u32[]{:S(2)}, u32[]{:S(2)}) collective-permute-start(f32[32,128]{1,0:T(8,128)S(1)} %copy.27), channel_id=1, source_target_pairs={{0,1},{1,2},{2,3},{3,4},{4,5},{5,6},{6,7},{7,8},{8,9},{9,10},{10,1... | collective-permute-start | bytes 49160 | tf_op jit(solution)/shard_map/while/body/eval_jaxpr/ppermute | solution.py:13
  1295.2 6.9 collective-permute-start
  1302.1 75.6 %collective-permute-start.1 = (f32[32,128]{1,0:T(8,128)S(1)}, f32[32,128]{1,0:T(8,128)S(1)}, u32[]{:S(2)}, u32[]{:S(2)}) collective-permute-start(f32[32,128]{1,0:T(8,128)S(1)} %copy.27), channel_id=1, source_target_pairs={{0,1},{1,2},{2,3},{3,4},{4,5},{5,6},{6,7},{7,8},{8,9},{9,10},{10,1... | collective-permute-start | bytes 49160 | tf_op jit(solution)/shard_map/while/body/eval_jaxpr/ppermute | solution.py:13
  1375.7 6.9 collective-permute-start
  1382.6 0.7 copy-start.1
Sparse Core Ops, SparseCore 0:
  14.5 67.8 reduce-scatter.1
where the time goes:
time: 1390 us
  blocking collectives  1070 us (77%)
  waiting for transfers between devices  146 us (11%)
  starting transfers between devices  61.3 us (4%)
  matrix products  45.5 us (3%)
  loops' own time  32.3 us (2%)
  between operations  14.1 us (1%)
    psum x16, blocking collectives, run_section(): gradient = lax.psum(local_grad, 'samp')  1070 us
    ppermute x32, waiting for transfers between devices, from_behind(): return lax.ppermute(value, axis, pairs)  78.4 us
    reduce_scatter x1, waiting for transfers between devices, per_device(): lax.psum_scatter(partial_sum, 'feat', scatter_dimension=0, tiled=True)  68.1 us
    ppermute x32, starting transfers between devices, from_behind(): return lax.ppermute(value, axis, pairs)  61.3 us
    another operation x1, loops' own time, per_device(): lax.fori_loop(0, cycle_size, run_section, (blocks, residual, weight))  32.3 us
  transfers between devices with their start and end apart: 33, of which 17 were waited for; matrix products, arithmetic and copies ran while one was open for 4% of the time, Pallas kernels for 0%

commit v1 on v0

v1 whole, which is shorter than its diff:
```python
import functools

import jax
import jax.numpy as jnp
from jax import lax
from jax.experimental import pallas as pl
from jax.experimental.pallas import tpu as pltpu
from jax.sharding import PartitionSpec as P

MESH = pl.DeviceIdType.MESH
EXACT = lax.Precision.HIGHEST
L1 = 0.25
SLAB = 16


def nt_dot(a, b, precision=None):
    return lax.dot_general(
        a, b, (((1,), (1,)), ((), ())), precision=precision, preferred_element_type=jnp.float32
    )


def window_kernel(
    n_samp,
    n_feat,
    n_tiles,
    rows_ref,
    cols_ref,
    cols_smem,
    order_smem,
    labels_hbm,
    beta_hbm,
    vals_hbm,
    hess_hbm,
    beta_out,
    res_out,
    labels_v,
    beta_v,
    vals,
    hess,
    ids,
    partial,
    m_recv,
    g_send,
    g_recv,
    r_send,
    r_buf,
    w_buf,
    shrunk_all,
    load_sem,
    m_send_sem,
    m_recv_sem,
    g_send_sem,
    g_recv_sem,
    r_send_sem,
    r_recv_sem,
    w_send_sem,
    w_recv_sem,
):
    si = lax.axis_index("samp")
    fj = lax.axis_index("feat")
    group = labels_v.shape[0]
    edge = vals.shape[-1]
    right = lax.rem(fj + 1, n_feat)

    own_rows = pl.ds(pl.multiple_of(fj * group, group), group)
    loads = [
        pltpu.make_async_copy(vals_hbm, vals, load_sem.at[0]),
        pltpu.make_async_copy(beta_hbm, beta_v, load_sem.at[1]),
        pltpu.make_async_copy(labels_hbm.at[own_rows], labels_v, load_sem.at[2]),
        pltpu.make_async_copy(hess_hbm, hess, load_sem.at[3]),
    ]
    for load in loads:
        load.start()

    barrier = pltpu.get_barrier_semaphore()
    for d in range(1, n_samp):
        pl.semaphore_signal(
            barrier, inc=1, device_id=(lax.rem(si + d, n_samp), fj), device_id_type=MESH
        )
    for d in range(1, n_feat):
        pl.semaphore_signal(
            barrier, inc=1, device_id=(si, lax.rem(fj + d, n_feat)), device_id_type=MESH
        )

    ids[...] = jnp.full(ids.shape, -1, jnp.int32)
    ids[0:1, 0:n_tiles] = rows_ref[...]
    ids[1:2, 0:n_tiles] = cols_ref[...]
    row_id = ids[0:1, :]
    col_id = ids[1:2, :]
    tile_section = lax.rem(fj - lax.shift_right_arithmetic(row_id, group.bit_length() - 1) + 2 * n_feat, n_feat)
    offset_row = jnp.bitwise_and(row_id, group - 1)
    section_row = jnp.full(row_id.shape, -1, jnp.int32)
    for s in range(n_feat):
        hit = (tile_section == s) & (col_id == order_smem[0, s])
        section_row = jnp.where(hit, s, section_row)
    offset_col = jnp.transpose(jnp.broadcast_to(offset_row, (edge, edge)))[:n_tiles, :group]
    section_col = jnp.transpose(jnp.broadcast_to(section_row, (edge, edge)))[:n_tiles, :group]
    offset_row = jnp.broadcast_to(offset_row[:, :n_tiles], (group, n_tiles))
    section_row = jnp.broadcast_to(section_row[:, :n_tiles], (group, n_tiles))
    same_col = offset_col == lax.broadcasted_iota(jnp.int32, (n_tiles, group), 1)
    same_row = offset_row == lax.broadcasted_iota(jnp.int32, (group, n_tiles), 0)
    sub = lax.broadcasted_iota(jnp.int32, (SLAB, edge), 0)
    slabs = n_tiles // SLAB

    def tile_images(lhs):
        out = []
        for m in range(slabs):
            acc = jnp.zeros((SLAB, edge), jnp.float32)
            for t in range(SLAB):
                acc = jnp.where(sub == t, nt_dot(lhs[m], vals[m * SLAB + t]), acc)
            out.append(acc)
        return jnp.concatenate(out, axis=0)

    loads[0].wait()
    loads[1].wait()
    picked = []
    for m in range(slabs):
        acc = jnp.zeros((SLAB, edge), jnp.float32)
        for t in range(SLAB):
            row = beta_v[pl.ds(cols_smem[0, m * SLAB + t], 1), :]
            acc = jnp.where(sub == t, jnp.broadcast_to(row, (SLAB, edge)), acc)
        picked.append(acc.astype(jnp.bfloat16))
    products = tile_images(picked)
    row_blocks = partial.shape[0] * group
    placing = jnp.broadcast_to(ids[0:1, 0:n_tiles], (row_blocks, n_tiles)) == lax.broadcasted_iota(
        jnp.int32, (row_blocks, n_tiles), 0
    )
    sums = jnp.dot(placing.astype(jnp.float32), products, precision=EXACT)
    partial[...] = sums.reshape(partial.shape)

    pl.semaphore_wait(barrier, n_samp + n_feat - 2)
    for d in range(1, n_feat):
        peer = lax.rem(fj + d, n_feat)
        pltpu.make_async_remote_copy(
            src_ref=partial.at[peer],
            dst_ref=m_recv.at[fj],
            send_sem=m_send_sem,
            recv_sem=m_recv_sem,
            device_id=(si, peer),
            device_id_type=MESH,
        ).start()
    m_recv[fj] = partial[fj]
    fifteen = m_recv.at[pl.ds(0, n_feat - 1)]
    pltpu.make_async_copy(fifteen, fifteen, m_recv_sem).wait()
    margin = m_recv[0]
    for d in range(1, n_feat):
        margin = margin + m_recv[d]
    prob = 1.0 / (1.0 + jnp.exp(-margin))
    loads[2].wait()
    w_buf[0] = prob * (1.0 - prob)
    r_buf[0] = labels_v[...].astype(jnp.float32) - prob

    def shift(buf_src, buf_dst, send_sem, recv_sem):
        return pltpu.make_async_remote_copy(
            src_ref=buf_src,
            dst_ref=buf_dst,
            send_sem=send_sem,
            recv_sem=recv_sem,
            device_id=(si, right),
            device_id_type=MESH,
        )

    shift(w_buf.at[0], w_buf.at[1], w_send_sem, w_recv_sem.at[1]).start()
    loads[3].wait()

    def section(s, carry):
        residual = r_buf[s]
        chosen = (same_col & (section_col == s)).astype(jnp.bfloat16)
        tiles = jnp.dot(
            chosen, residual.astype(jnp.bfloat16), preferred_element_type=jnp.float32
        ).astype(jnp.bfloat16)
        lhs = []
        for k in range(n_tiles):
            m, t = k // SLAB, k % SLAB
            lhs.append(
                jnp.where(sub == t, tiles[m * SLAB : (m + 1) * SLAB], jnp.zeros((), jnp.bfloat16))
            )
        grads = jnp.dot(
            jnp.concatenate(lhs, axis=1),
            vals[...].reshape(n_tiles * edge, edge),
            preferred_element_type=jnp.float32,
        )
        local = jnp.sum(grads, axis=0, keepdims=True)
        g_send[s] = local
        for d in list(range(1, n_samp)):
            pltpu.make_async_remote_copy(
                src_ref=g_send.at[s],
                dst_ref=g_recv.at[s, si],
                send_sem=g_send_sem,
                recv_sem=g_recv_sem.at[s],
                device_id=(lax.rem(si + d, n_samp), fj),
                device_id_type=MESH,
            ).start()
        g_recv[s, si] = local

        @pl.when(s < n_feat - 1)
        def _():
            shift(w_buf.at[s], w_buf.at[s + 1], w_send_sem, w_recv_sem.at[s + 1]).wait_recv()

        @pl.when(s < n_feat - 2)
        def _():
            shift(w_buf.at[s + 1], w_buf.at[s + 2], w_send_sem, w_recv_sem.at[s + 2]).start()

        current = beta_v[pl.ds(order_smem[0, s], 1), :]
        others = g_recv.at[s, pl.ds(0, n_samp - 1)]
        pltpu.make_async_copy(others, others, g_recv_sem.at[s]).wait()
        gradient = g_recv[s, 0]
        for i in range(1, n_samp):
            gradient = gradient + g_recv[s, i]
        step = nt_dot(jnp.broadcast_to(gradient, (8, edge)), hess[s], EXACT)[0:1, :]
        moved = current + step
        shrunk = jnp.where(moved > L1, moved - L1, jnp.where(moved < -L1, moved + L1, 0.0))
        shrunk_all[s] = shrunk
        change = jnp.broadcast_to(shrunk - current, (SLAB, edge)).astype(jnp.bfloat16)
        image = tile_images([change] * slabs)
        chosen_t = (same_row & (section_row == s)).astype(jnp.float32)
        landed = jnp.dot(chosen_t, image, precision=EXACT)
        r_send[s] = residual - w_buf[s] * landed
        copy = shift(r_send.at[s], r_buf.at[s + 1], r_send_sem, r_recv_sem.at[s + 1])
        copy.start()
        copy.wait_recv()
        return carry

    lax.fori_loop(0, n_feat, section, 0)

    res_out[...] = r_buf[n_feat]
    blocks = beta_v[...]
    block_ids = lax.broadcasted_iota(jnp.int32, blocks.shape, 0)
    for s in range(n_feat):
        blocks = jnp.where(
            block_ids == order_smem[0, s], jnp.broadcast_to(shrunk_all[s], blocks.shape), blocks
        )
    beta_out[...] = blocks

    pltpu.make_async_copy(fifteen, fifteen, m_send_sem).wait()
    sent = g_recv.at[:, pl.ds(0, n_samp - 1)]
    pltpu.make_async_copy(sent, sent, g_send_sem).wait()
    sent_r = r_buf.at[pl.ds(0, n_feat)]
    pltpu.make_async_copy(sent_r, sent_r, r_send_sem).wait()
    sent_w = w_buf.at[pl.ds(0, n_feat - 1)]
    pltpu.make_async_copy(sent_w, sent_w, w_send_sem).wait()


def per_device(n_samp, n_feat, labels, beta, tile_rows, tile_cols, tile_values, block_order, hess_inv):
    n_tiles, edge = tile_values.shape[2], tile_values.shape[-1]
    row_blocks = labels.shape[0] // edge
    feat_blocks = beta.shape[0] // edge
    group = row_blocks // n_feat
    vmem = pl.BlockSpec(memory_space=pltpu.VMEM)
    smem = pl.BlockSpec(memory_space=pltpu.SMEM)
    anywhere = pl.BlockSpec(memory_space=pl.ANY)
    f32 = jnp.float32
    dma = pltpu.SemaphoreType.DMA
    rows = tile_rows.reshape(1, n_tiles)
    cols = tile_cols.reshape(1, n_tiles)
    beta_new, residual = pl.pallas_call(
        functools.partial(window_kernel, n_samp, n_feat, n_tiles),
        out_shape=(
            jax.ShapeDtypeStruct((feat_blocks, edge), f32),
            jax.ShapeDtypeStruct((group, edge), f32),
        ),
        in_specs=[vmem, vmem, smem, smem, anywhere, anywhere, anywhere, anywhere],
        out_specs=(vmem, vmem),
        scratch_shapes=[
            pltpu.VMEM((group, edge), jnp.int32),
            pltpu.VMEM((feat_blocks, edge), f32),
            pltpu.VMEM((n_tiles, edge, edge), jnp.bfloat16),
            pltpu.VMEM((n_feat, edge, edge), f32),
            pltpu.VMEM((8, edge), jnp.int32),
            pltpu.VMEM((n_feat, group, edge), f32),
            pltpu.VMEM((n_feat, group, edge), f32),
            pltpu.VMEM((n_feat, 1, edge), f32),
            pltpu.VMEM((n_feat, n_samp, 1, edge), f32),
            pltpu.VMEM((n_feat, group, edge), f32),
            pltpu.VMEM((n_feat + 1, group, edge), f32),
            pltpu.VMEM((n_feat, group, edge), f32),
            pltpu.VMEM((n_feat, 1, edge), f32),
            dma((4,)),
            dma(()),
            dma(()),
            dma(()),
            dma((n_feat,)),
            dma(()),
            dma((n_feat + 1,)),
            dma(()),
            dma((n_feat,)),
        ],
        compiler_params=pltpu.CompilerParams(collective_id=0, has_side_effects=True),
    )(
        rows,
        cols,
        cols,
        block_order,
        labels.reshape(row_blocks, edge),
        beta.reshape(feat_blocks, edge),
        tile_values.reshape(n_tiles, edge, edge),
        hess_inv.reshape(n_feat, edge, edge),
    )
    return beta_new.reshape(-1), residual.reshape(-1)


def solution(mesh):
    placed = (
        P("samp"),
        P("feat"),
        P("samp", "feat", None),
        P("samp", "feat", None),
        P("samp", "feat", None, None, None),
        P("feat", None),
        P("feat", None, None, None),
    )
    return jax.shard_map(
        functools.partial(per_device, mesh.shape["samp"], mesh.shape["feat"]),
        mesh=mesh,
        in_specs=placed,
        out_specs=(P("feat"), P(("samp", "feat"))),
        check_vma=False,
    )
```

time: 1390 us -> 204 us (0.15)
  blocking collectives: 1070 us -> 0 us
  Pallas kernels: 0 us -> 200 us
  waiting for transfers between devices: 146 us -> 0 us
  starting transfers between devices: 61.3 us -> 0 us
  matrix products: 45.5 us -> 0 us
  loops' own time: 32.3 us -> 0 us
    psum x16 -> x0, blocking collectives: 1070 us -> none  [run_section(): gradient = lax.psum(local_grad, 'samp')]
    pallas_call x0 -> x1, Pallas kernels: none -> 200 us  [per_device(): pl.pallas_call(functools.partial(window_kernel, n_samp, n_feat, n_tiles),...]
    ppermute x32 -> x0, waiting for transfers between devices: 78.4 us -> none  [from_behind(): return lax.ppermute(value, axis, pairs)]
    reduce_scatter x1 -> x0, waiting for transfers between devices: 68.1 us -> none  [per_device(): lax.psum_scatter(partial_sum, 'feat', scatter_dimension=0, tiled=True)]
    ppermute x32 -> x0, starting transfers between devices: 61.3 us -> none  [from_behind(): return lax.ppermute(value, axis, pairs)]
    dot_general x82 -> x0, matrix products: 45.5 us -> none  [the longest x16 16.5 us: run_section(): moved_block = current + jnp.dot(inverse, gradient, precision=exact_prec)]
    another operation x1 -> x0, loops' own time: 32.3 us -> none  [per_device(): lax.fori_loop(0, cycle_size, run_section, (blocks, residual, weight))]
  transfers between devices with their start and end apart: 33 -> 0, of which waited for: 17 -> 0; matrix products, arithmetic and copies ran while one was open for 4% -> 0% of each run, Pallas kernels for 0% -> 0%
where the time goes in v1:
time: 204 us
  Pallas kernels  200 us (98%)
  local copies, waits for them, and re-layouts  2.99 us (1%)
    pallas_call x1, Pallas kernels, per_device(): pl.pallas_call(functools.partial(window_kernel, n_samp, n_feat, n_tiles),...  200 us

profile of v1, /device:TPU:1, one launch (start us, length us, event | category | flops | bytes accessed | tf_op | source)
XLA Modules:
  0.0 204.0 jit_solution(13016723618602705748)
XLA Ops:
  0.6 200.4 %shard_map.86 = (f32[512,128]{1,0:T(8,128)}, f32[32,128]{1,0:T(8,128)}) custom-call(s32[1,64]{1,0:T(1,128)} %bitcast.16, s32[1,64]{1,0:T(1,128)} %bitcast.14, s32[1,64]{1,0:T(1,128)} %bitcast.15, s32[1,16]{1,0:T(1,128)} %order_smem.1, s32[512,128]{1,0:T(8,128)} %bitcast.10, f32[512,128]{1,0:T(8,128)} %bitcast.11, bf16[64,128,128]{2,1,0:T(8,128)(2,1)} %bitcast.8, ...), custom_call_target="tpu_custom_call" | custom-call | tf_op jit(solution)/shard_map/pallas_call | solution.py:256
  201.1 1.7 copy.11
  202.7 1.3 copy.12

commit v2 on v1

v2 whole, which is shorter than its diff:
```python
import functools

import jax
import jax.numpy as jnp
from jax import lax
from jax.experimental import pallas as pl
from jax.experimental.pallas import tpu as pltpu
from jax.sharding import PartitionSpec as P

MESH = pl.DeviceIdType.MESH
L1 = 0.25
SLAB = 16
BF16 = jnp.bfloat16
F32 = jnp.float32


def nt_dot(a, b):
    return lax.dot_general(a, b, (((1,), (1,)), ((), ())), preferred_element_type=F32)


def three_parts(x):
    high = x.astype(BF16)
    rest = x - high.astype(F32)
    middle = rest.astype(BF16)
    low = (rest - middle.astype(F32)).astype(BF16)
    return high, middle, low


def tree_sum(terms):
    while len(terms) > 1:
        terms = [a + b for a, b in zip(terms[::2], terms[1::2])] + terms[len(terms) // 2 * 2 :]
    return terms[0]


def window_kernel(
    n_samp,
    n_feat,
    n_tiles,
    rows_ref,
    cols_ref,
    cols_smem,
    order_smem,
    labels_hbm,
    beta_hbm,
    vals_hbm,
    hess_hbm,
    beta_out,
    res_out,
    labels_v,
    vals,
    hess,
    hess_t,
    ids,
    index_v,
    index_s,
    prefix,
    prefix_t,
    dense,
    dense_t,
    shrunk_all,
    partial,
    m_recv,
    g_send,
    g_recv,
    r_send,
    r_buf,
    w_buf,
    load_sem,
    index_sem,
    m_send_sem,
    m_recv_sem,
    g_send_sem,
    g_recv_sem,
    r_send_sem,
    r_recv_sem,
    w_send_sem,
    w_recv_sem,
):
    si = lax.axis_index("samp")
    fj = lax.axis_index("feat")
    group = labels_v.shape[0]
    shift_bits = group.bit_length() - 1
    edge = vals.shape[-1]
    slabs = n_tiles // SLAB
    right = lax.rem(fj + 1, n_feat)
    row_blocks = n_feat * group
    starts = row_blocks + edge

    own_rows = pl.ds(pl.multiple_of(fj * group, group), group)
    loads = [
        pltpu.make_async_copy(vals_hbm, vals, load_sem.at[0]),
        pltpu.make_async_copy(beta_hbm, beta_out, load_sem.at[1]),
        pltpu.make_async_copy(labels_hbm.at[own_rows], labels_v, load_sem.at[2]),
        pltpu.make_async_copy(hess_hbm, hess, load_sem.at[3]),
    ]
    for load in loads:
        load.start()

    barrier = pltpu.get_barrier_semaphore()
    for d in range(1, n_samp):
        pl.semaphore_signal(
            barrier, inc=1, device_id=(lax.rem(si + d, n_samp), fj), device_id_type=MESH
        )
    for d in range(1, n_feat):
        pl.semaphore_signal(
            barrier, inc=1, device_id=(si, lax.rem(fj + d, n_feat)), device_id_type=MESH
        )

    last = 2 * row_blocks
    ids[...] = jnp.full(ids.shape, -1, jnp.int32)
    ids[0:1, 0:n_tiles] = rows_ref[...]
    ids[1:2, 0:n_tiles] = cols_ref[...]
    row_id, col_id = ids[0:1, :], ids[1:2, :]
    section = lax.rem(fj - lax.shift_right_arithmetic(row_id, shift_bits) + 2 * n_feat, n_feat)
    code = jnp.full(row_id.shape, last, jnp.int32)
    for s in range(n_feat):
        hit = (section == s) & (col_id == order_smem[0, s])
        code = jnp.where(hit, s * group + jnp.bitwise_and(row_id, group - 1), code)

    def down(row):
        return jnp.transpose(jnp.broadcast_to(row, (edge, edge)))

    lane = lax.broadcasted_iota(jnp.int32, (1, edge), 1)
    across = lax.broadcasted_iota(jnp.int32, (edge, edge), 1)
    along = lax.broadcasted_iota(jnp.int32, (edge, edge), 0)
    code_down = down(code)
    for b in range(starts // edge):
        before = (code_down < across + b * edge).astype(jnp.int32)
        index_v[0:1, b * edge : (b + 1) * edge] = jnp.sum(before, axis=0, keepdims=True)
    key = code * edge + lane
    rank = jnp.sum((down(key) < key).astype(jnp.int32), axis=0, keepdims=True)
    index_v[0:1, starts : starts + edge] = jnp.sum(
        jnp.where(down(rank) == across, along, 0), axis=0, keepdims=True
    )
    index_copy = pltpu.make_async_copy(index_v, index_s, index_sem)
    index_copy.start()

    sub = lax.broadcasted_iota(jnp.int32, (SLAB, edge), 0)
    row_is = [(sub == t).astype(F32).astype(BF16) for t in range(SLAB)]

    def set_prefixes():
        prefix[0] = jnp.zeros((edge, edge), F32)
        prefix_t[0] = jnp.zeros((edge, edge), F32)
        eye = (along == across).astype(F32).astype(BF16)

        def add_tile(n, carry):
            tile = vals[index_s[0, starts + n]]
            prefix[n + 1] = prefix[n] + tile.astype(F32)
            prefix_t[n + 1] = prefix_t[n] + nt_dot(eye, tile)
            return carry

        lax.fori_loop(0, n_tiles, add_tile, 0)

    def set_dense(s, source, out):
        for g in range(group):
            at = s * group + g
            out[g] = (source[index_s[0, at + 1]] - source[index_s[0, at]]).astype(BF16)

    def set_hessian(s):
        for p, part in enumerate(three_parts(jnp.transpose(hess[s]))):
            hess_t[pl.ds(p * edge, edge)] = part

    def set_block(s):
        blocks = beta_out[...]
        block_ids = lax.broadcasted_iota(jnp.int32, blocks.shape, 0)
        beta_out[...] = jnp.where(
            block_ids == order_smem[0, s], jnp.broadcast_to(shrunk_all[s], blocks.shape), blocks
        )

    loads[0].wait()
    loads[1].wait()
    products = []
    for m in range(slabs):
        acc = jnp.zeros((SLAB, edge), F32)
        for t in range(SLAB):
            row = beta_out[pl.ds(cols_smem[0, m * SLAB + t], 1), :]
            acc = jnp.where(sub == t, jnp.broadcast_to(row, (SLAB, edge)), acc)
        picked = acc.astype(BF16)
        acc = jnp.zeros((SLAB, edge), F32)
        for t in range(SLAB):
            acc = jnp.where(sub == t, nt_dot(picked, vals[m * SLAB + t]), acc)
        products.append(acc)
    placing = (
        jnp.broadcast_to(ids[0:1, 0:n_tiles], (row_blocks, n_tiles))
        == lax.broadcasted_iota(jnp.int32, (row_blocks, n_tiles), 0)
    ).astype(F32).astype(BF16)
    parts = three_parts(jnp.concatenate(products, axis=0))
    sums = jnp.dot(placing, parts[0], preferred_element_type=F32)
    for part in parts[1:]:
        sums = sums + jnp.dot(placing, part, preferred_element_type=F32)
    partial[...] = sums.reshape(partial.shape)

    pl.semaphore_wait(barrier, n_samp + n_feat - 2)
    for d in [x for y in range(n_feat // 2, 0, -1) for x in sorted({y, n_feat - y})]:
        peer = lax.rem(fj + d, n_feat)
        pltpu.make_async_remote_copy(
            src_ref=partial.at[peer],
            dst_ref=m_recv.at[fj],
            send_sem=m_send_sem,
            recv_sem=m_recv_sem,
            device_id=(si, peer),
            device_id_type=MESH,
        ).start()
    m_recv[fj] = partial[fj]
    loads[2].wait()
    loads[3].wait()
    set_hessian(0)
    index_copy.wait()
    set_prefixes()
    set_dense(0, prefix, dense)
    set_dense(0, prefix_t, dense_t)
    fifteen = m_recv.at[pl.ds(0, n_feat - 1)]
    pltpu.make_async_copy(fifteen, fifteen, m_recv_sem).wait()
    margin = tree_sum([m_recv[d] for d in range(n_feat)])
    prob = 1.0 / (1.0 + jnp.exp(-margin))
    w_buf[0] = prob * (1.0 - prob)
    r_buf[0] = labels_v[...].astype(F32) - prob

    def shift(buf_src, buf_dst, send_sem, recv_sem):
        return pltpu.make_async_remote_copy(
            src_ref=buf_src,
            dst_ref=buf_dst,
            send_sem=send_sem,
            recv_sem=recv_sem,
            device_id=(si, right),
            device_id_type=MESH,
        )

    shift(w_buf.at[0], w_buf.at[1], w_send_sem, w_recv_sem.at[1]).start()

    peers = sorted(
        ((x, y, c) for x in range(2) for y in range(n_samp // 4) for c in range(2)),
        key=lambda o: -(2 * o[0] + min(o[1], n_samp // 4 - o[1]) + 0.3 * o[2]),
    )[:-1]
    half = n_samp // 2
    my_x, my_y, my_c = si // half, lax.rem(si // 2, n_samp // 4), lax.rem(si, 2)

    def section(s, carry):
        rounded = r_buf[s].astype(BF16)
        picks = jnp.concatenate(
            [
                row_is[g % SLAB] * rounded[g // SLAB * SLAB : (g // SLAB + 1) * SLAB]
                for g in range(group)
            ],
            axis=1,
        )
        grads = jnp.dot(picks, dense[...].reshape(group * edge, edge), preferred_element_type=F32)
        local = jnp.sum(grads, axis=0, keepdims=True)
        g_send[s] = local
        for dx, dy, dc in peers:
            peer = (
                lax.rem(my_x + dx, 2) * half
                + lax.rem(my_y + dy, n_samp // 4) * 2
                + lax.rem(my_c + dc, 2)
            )
            pltpu.make_async_remote_copy(
                src_ref=g_send.at[s],
                dst_ref=g_recv.at[s, si],
                send_sem=g_send_sem,
                recv_sem=g_recv_sem.at[s],
                device_id=(peer, fj),
                device_id_type=MESH,
            ).start()
        g_recv[s, si] = local

        @pl.when(s < n_feat - 1)
        def _():
            shift(w_buf.at[s], w_buf.at[s + 1], w_send_sem, w_recv_sem.at[s + 1]).wait_recv()
            set_dense(s + 1, prefix, dense)

        @pl.when(s > 0)
        def _():
            set_block(s - 1)

        @pl.when(s < n_feat - 2)
        def _():
            shift(w_buf.at[s + 1], w_buf.at[s + 2], w_send_sem, w_recv_sem.at[s + 2]).start()

        target = order_smem[0, s]
        current = beta_out[pl.ds(target, 1), :]
        others = g_recv.at[s, pl.ds(0, n_samp - 1)]
        pltpu.make_async_copy(others, others, g_recv_sem.at[s]).wait()
        gradient = tree_sum([g_recv[s, i] for i in range(n_samp)])
        high, middle, low = [
            jnp.broadcast_to(part.astype(F32), (SLAB, edge)) for part in three_parts(gradient)
        ]
        stacked = jnp.where(
            sub == 0, high, jnp.where(sub == 1, middle, jnp.where(sub == 2, low, 0.0))
        ).astype(BF16)
        products = jnp.dot(
            jnp.concatenate([stacked] * 3, axis=1), hess_t[...], preferred_element_type=F32
        )
        moved = current + jnp.sum(products, axis=0, keepdims=True)
        shrunk = jnp.where(moved > L1, moved - L1, jnp.where(moved < -L1, moved + L1, 0.0))
        shrunk_all[s] = shrunk
        change = jnp.broadcast_to(shrunk - current, (SLAB, edge)).astype(BF16)
        spread = jnp.concatenate([row_is[t] * change for t in range(SLAB)], axis=1)
        landed = jnp.concatenate(
            [
                jnp.dot(
                    spread,
                    dense_t[pl.ds(m * SLAB, SLAB)].reshape(SLAB * edge, edge),
                    preferred_element_type=F32,
                )
                for m in range(group // SLAB)
            ],
            axis=0,
        )
        r_send[s] = r_buf[s] - w_buf[s] * landed
        copy = shift(r_send.at[s], r_buf.at[s + 1], r_send_sem, r_recv_sem.at[s + 1])
        copy.start()

        @pl.when(s < n_feat - 1)
        def _():
            set_hessian(s + 1)
            set_dense(s + 1, prefix_t, dense_t)

        copy.wait_recv()
        return carry

    lax.fori_loop(0, n_feat, section, 0)

    set_block(n_feat - 1)
    res_out[...] = r_buf[n_feat]

    pltpu.make_async_copy(fifteen, fifteen, m_send_sem).wait()
    sent = g_recv.at[:, pl.ds(0, n_samp - 1)]
    pltpu.make_async_copy(sent, sent, g_send_sem).wait()
    sent_r = r_buf.at[pl.ds(0, n_feat)]
    pltpu.make_async_copy(sent_r, sent_r, r_send_sem).wait()
    sent_w = w_buf.at[pl.ds(0, n_feat - 1)]
    pltpu.make_async_copy(sent_w, sent_w, w_send_sem).wait()


def per_device(n_samp, n_feat, labels, beta, tile_rows, tile_cols, tile_values, block_order, hess_inv):
    n_tiles, edge = tile_values.shape[2], tile_values.shape[-1]
    row_blocks = labels.shape[0] // edge
    feat_blocks = beta.shape[0] // edge
    group = row_blocks // n_feat
    vmem = pl.BlockSpec(memory_space=pltpu.VMEM)
    smem = pl.BlockSpec(memory_space=pltpu.SMEM)
    anywhere = pl.BlockSpec(memory_space=pl.ANY)
    dma = pltpu.SemaphoreType.DMA
    beta_new, residual = pl.pallas_call(
        functools.partial(window_kernel, n_samp, n_feat, n_tiles),
        out_shape=(
            jax.ShapeDtypeStruct((feat_blocks, edge), F32),
            jax.ShapeDtypeStruct((group, edge), F32),
        ),
        in_specs=[vmem, vmem, smem, smem, anywhere, anywhere, anywhere, anywhere],
        out_specs=(vmem, vmem),
        scratch_shapes=[
            pltpu.VMEM((group, edge), jnp.int32),
            pltpu.VMEM((n_tiles, edge, edge), BF16),
            pltpu.VMEM((n_feat, edge, edge), F32),
            pltpu.VMEM((3 * edge, edge), BF16),
            pltpu.VMEM((8, edge), jnp.int32),
            pltpu.VMEM((1, row_blocks + 2 * edge), jnp.int32),
            pltpu.SMEM((1, row_blocks + 2 * edge), jnp.int32),
            pltpu.VMEM((n_tiles + 1, edge, edge), F32),
            pltpu.VMEM((n_tiles + 1, edge, edge), F32),
            pltpu.VMEM((group, edge, edge), BF16),
            pltpu.VMEM((group, edge, edge), BF16),
            pltpu.VMEM((n_feat, 1, edge), F32),
            pltpu.VMEM((n_feat, group, edge), F32),
            pltpu.VMEM((n_feat, group, edge), F32),
            pltpu.VMEM((n_feat, 1, edge), F32),
            pltpu.VMEM((n_feat, n_samp, 1, edge), F32),
            pltpu.VMEM((n_feat, group, edge), F32),
            pltpu.VMEM((n_feat + 1, group, edge), F32),
            pltpu.VMEM((n_feat, group, edge), F32),
            dma((4,)),
            dma(()),
            dma(()),
            dma(()),
            dma(()),
            dma((n_feat,)),
            dma(()),
            dma((n_feat + 1,)),
            dma(()),
            dma((n_feat,)),
        ],
        compiler_params=pltpu.CompilerParams(collective_id=0, has_side_effects=True),
    )(
        tile_rows.reshape(1, n_tiles),
        tile_cols.reshape(1, n_tiles),
        tile_cols.reshape(1, n_tiles),
        block_order,
        labels.reshape(row_blocks, edge),
        beta.reshape(feat_blocks, edge),
        tile_values.reshape(n_tiles, edge, edge),
        hess_inv.reshape(n_feat, edge, edge),
    )
    return beta_new.reshape(-1), residual.reshape(-1)


def solution(mesh):
    placed = (
        P("samp"),
        P("feat"),
        P("samp", "feat", None),
        P("samp", "feat", None),
        P("samp", "feat", None, None, None),
        P("feat", None),
        P("feat", None, None, None),
    )
    return jax.shard_map(
        functools.partial(per_device, mesh.shape["samp"], mesh.shape["feat"]),
        mesh=mesh,
        in_specs=placed,
        out_specs=(P("feat"), P(("samp", "feat"))),
        check_vma=False,
    )
```

time: 204 us -> 180 us (0.88)
  Pallas kernels: 200 us -> 176 us
    pallas_call x1, Pallas kernels: 200 us -> 176 us  [per_device(): pl.pallas_call(functools.partial(window_kernel, n_samp, n_feat, n_tiles),...]
where the time goes in v2:
time: 180 us; the launch traced here: 179 us
  Pallas kernels  176 us (98%)
  local copies, waits for them, and re-layouts  2.99 us (2%)
    pallas_call x1, Pallas kernels, per_device(): pl.pallas_call(functools.partial(window_kernel, n_samp, n_feat, n_tiles),...  176 us

profile of v2, /device:TPU:1, one launch (start us, length us, event | category | flops | bytes accessed | tf_op | source)
XLA Modules:
  0.0 179.5 jit_solution(13067859361385033309)
XLA Ops:
  0.6 175.8 %shard_map.86 = (f32[512,128]{1,0:T(8,128)}, f32[32,128]{1,0:T(8,128)}) custom-call(s32[1,64]{1,0:T(1,128)} %bitcast.16, s32[1,64]{1,0:T(1,128)} %bitcast.14, s32[1,64]{1,0:T(1,128)} %bitcast.15, s32[1,16]{1,0:T(1,128)} %order_smem.1, s32[512,128]{1,0:T(8,128)} %bitcast.10, f32[512,128]{1,0:T(8,128)} %bitcast.11, bf16[64,128,128]{2,1,0:T(8,128)(2,1)} %bitcast.8, ...), custom_call_target="tpu_custom_call" | custom-call | tf_op jit(solution)/shard_map/pallas_call | solution.py:344
  176.5 1.7 copy.11
  178.1 1.3 copy.12

commit v3 on v2

--- a/solution.py
+++ b/solution.py
@@ -9,6 +9,7 @@
 
 MESH = pl.DeviceIdType.MESH
 L1 = 0.25
+UNROLL = 8
 SLAB = 16
 BF16 = jnp.bfloat16
 F32 = jnp.float32
@@ -24,6 +25,14 @@
     middle = rest.astype(BF16)
     low = (rest - middle.astype(F32)).astype(BF16)
     return high, middle, low
+
+
+def two_dots(a, b_ref):
+    half = b_ref.shape[0] // 2
+    return [
+        jnp.dot(a[:, rows], b_ref[rows], preferred_element_type=F32)
+        for rows in (slice(0, half), slice(half, 2 * half))
+    ]
 
 
 def tree_sum(terms):
@@ -47,6 +56,7 @@
     beta_out,
     res_out,
     labels_v,
+    beta_v,
     vals,
     hess,
     hess_t,
@@ -59,6 +69,8 @@
     dense_t,
     shrunk_all,
     partial,
+    x_recv,
+    m_send,
     m_recv,
     g_send,
     g_recv,
@@ -67,6 +79,8 @@
     w_buf,
     load_sem,
     index_sem,
+    x_send_sem,
+    x_recv_sem,
     m_send_sem,
     m_recv_sem,
     g_send_sem,
@@ -89,7 +103,7 @@
     own_rows = pl.ds(pl.multiple_of(fj * group, group), group)
     loads = [
         pltpu.make_async_copy(vals_hbm, vals, load_sem.at[0]),
-        pltpu.make_async_copy(beta_hbm, beta_out, load_sem.at[1]),
+        pltpu.make_async_copy(beta_hbm, beta_v, load_sem.at[1]),
         pltpu.make_async_copy(labels_hbm.at[own_rows], labels_v, load_sem.at[2]),
         pltpu.make_async_copy(hess_hbm, hess, load_sem.at[3]),
     ]
@@ -137,33 +151,42 @@
 
     sub = lax.broadcasted_iota(jnp.int32, (SLAB, edge), 0)
     row_is = [(sub == t).astype(F32).astype(BF16) for t in range(SLAB)]
+    group_is = [jnp.concatenate([mask] * (group // SLAB), axis=0) for mask in row_is]
 
     def set_prefixes():
         prefix[0] = jnp.zeros((edge, edge), F32)
         prefix_t[0] = jnp.zeros((edge, edge), F32)
         eye = (along == across).astype(F32).astype(BF16)
 
-        def add_tile(n, carry):
-            tile = vals[index_s[0, starts + n]]
-            prefix[n + 1] = prefix[n] + tile.astype(F32)
-            prefix_t[n + 1] = prefix_t[n] + nt_dot(eye, tile)
+        def add_tiles(b, carry):
+            sums, sums_t = prefix[b * UNROLL], prefix_t[b * UNROLL]
+            for u in range(UNROLL):
+                n = b * UNROLL + u
+                tile = vals[index_s[0, starts + n]]
+                sums = sums + tile.astype(F32)
+                sums_t = sums_t + nt_dot(eye, tile)
+                prefix[n + 1] = sums
+                prefix_t[n + 1] = sums_t
             return carry
 
-        lax.fori_loop(0, n_tiles, add_tile, 0)
+        lax.fori_loop(0, n_tiles // UNROLL, add_tiles, 0)
 
     def set_dense(s, source, out):
         for g in range(group):
             at = s * group + g
-            out[g] = (source[index_s[0, at + 1]] - source[index_s[0, at]]).astype(BF16)
+            half, t = g // SLAB, g % SLAB
+            out[t * edge : (t + 1) * edge, half * edge : (half + 1) * edge] = (
+                source[index_s[0, at + 1]] - source[index_s[0, at]]
+            ).astype(BF16)
 
     def set_hessian(s):
         for p, part in enumerate(three_parts(jnp.transpose(hess[s]))):
             hess_t[pl.ds(p * edge, edge)] = part
 
     def set_block(s):
-        blocks = beta_out[...]
+        blocks = beta_v[...]
         block_ids = lax.broadcasted_iota(jnp.int32, blocks.shape, 0)
-        beta_out[...] = jnp.where(
+        beta_v[...] = jnp.where(
             block_ids == order_smem[0, s], jnp.broadcast_to(shrunk_all[s], blocks.shape), blocks
         )
 
@@ -173,7 +196,7 @@
     for m in range(slabs):
         acc = jnp.zeros((SLAB, edge), F32)
         for t in range(SLAB):
-            row = beta_out[pl.ds(cols_smem[0, m * SLAB + t], 1), :]
+            row = beta_v[pl.ds(cols_smem[0, m * SLAB + t], 1), :]
             acc = jnp.where(sub == t, jnp.broadcast_to(row, (SLAB, edge)), acc)
         picked = acc.astype(BF16)
         acc = jnp.zeros((SLAB, edge), F32)
@@ -191,17 +214,38 @@
     partial[...] = sums.reshape(partial.shape)
 
     pl.semaphore_wait(barrier, n_samp + n_feat - 2)
-    for d in [x for y in range(n_feat // 2, 0, -1) for x in sorted({y, n_feat - y})]:
-        peer = lax.rem(fj + d, n_feat)
-        pltpu.make_async_remote_copy(
-            src_ref=partial.at[peer],
-            dst_ref=m_recv.at[fj],
-            send_sem=m_send_sem,
-            recv_sem=m_recv_sem,
-            device_id=(si, peer),
+    n_z = n_feat // 2
+    fx, fz = fj // n_z, lax.rem(fj, n_z)
+    z_steps = sorted(range(n_z), key=lambda d: -min(d, n_z - d))
+
+    def across_x(k, d):
+        return pltpu.make_async_remote_copy(
+            src_ref=partial.at[(1 - fx) * n_z + lax.rem(fz + d, n_z)],
+            dst_ref=x_recv.at[k],
+            send_sem=x_send_sem,
+            recv_sem=x_recv_sem.at[k],
+            device_id=(si, (1 - fx) * n_z + fz),
             device_id_type=MESH,
-        ).start()
-    m_recv[fj] = partial[fj]
+        )
+
+    for k, d in enumerate(z_steps):
+        across_x(k, d).start()
+    for k, d in enumerate(z_steps):
+        owner = fx * n_z + lax.rem(fz + d, n_z)
+        across_x(k, d).wait_recv()
+        both = partial[owner] + x_recv[k]
+        if d == 0:
+            m_recv[fz] = both
+        else:
+            m_send[k] = both
+            pltpu.make_async_remote_copy(
+                src_ref=m_send.at[k],
+                dst_ref=m_recv.at[fz],
+                send_sem=m_send_sem,
+                recv_sem=m_recv_sem,
+                device_id=(si, owner),
+                device_id_type=MESH,
+            ).start()
     loads[2].wait()
     loads[3].wait()
     set_hessian(0)
@@ -209,9 +253,9 @@
     set_prefixes()
     set_dense(0, prefix, dense)
     set_dense(0, prefix_t, dense_t)
-    fifteen = m_recv.at[pl.ds(0, n_feat - 1)]
-    pltpu.make_async_copy(fifteen, fifteen, m_recv_sem).wait()
-    margin = tree_sum([m_recv[d] for d in range(n_feat)])
+    m_others = m_recv.at[pl.ds(0, n_z - 1)]
+    pltpu.make_async_copy(m_others, m_others, m_recv_sem).wait()
+    margin = tree_sum([m_recv[d] for d in range(n_z)])
     prob = 1.0 / (1.0 + jnp.exp(-margin))
     w_buf[0] = prob * (1.0 - prob)
     r_buf[0] = labels_v[...].astype(F32) - prob
@@ -237,15 +281,11 @@
 
     def section(s, carry):
         rounded = r_buf[s].astype(BF16)
-        picks = jnp.concatenate(
-            [
-                row_is[g % SLAB] * rounded[g // SLAB * SLAB : (g // SLAB + 1) * SLAB]
-                for g in range(group)
-            ],
-            axis=1,
-        )
-        grads = jnp.dot(picks, dense[...].reshape(group * edge, edge), preferred_element_type=F32)
-        local = jnp.sum(grads, axis=0, keepdims=True)
+        picks = jnp.concatenate([mask * rounded for mask in group_is], axis=1)
+        local = jnp.zeros((1, edge), F32)
+        for grads in two_dots(picks, dense):
+            both = grads[:SLAB, :edge] + grads[SLAB:, edge:]
+            local = local + jnp.sum(both, axis=0, keepdims=True)
         g_send[s] = local
         for dx, dy, dc in peers:
             peer = (
@@ -277,7 +317,7 @@
             shift(w_buf.at[s + 1], w_buf.at[s + 2], w_send_sem, w_recv_sem.at[s + 2]).start()
 
         target = order_smem[0, s]
-        current = beta_out[pl.ds(target, 1), :]
+        current = beta_v[pl.ds(target, 1), :]
         others = g_recv.at[s, pl.ds(0, n_samp - 1)]
         pltpu.make_async_copy(others, others, g_recv_sem.at[s]).wait()
         gradient = tree_sum([g_recv[s, i] for i in range(n_samp)])
@@ -295,41 +335,60 @@
         shrunk_all[s] = shrunk
         change = jnp.broadcast_to(shrunk - current, (SLAB, edge)).astype(BF16)
         spread = jnp.concatenate([row_is[t] * change for t in range(SLAB)], axis=1)
-        landed = jnp.concatenate(
-            [
-                jnp.dot(
-                    spread,
-                    dense_t[pl.ds(m * SLAB, SLAB)].reshape(SLAB * edge, edge),
-                    preferred_element_type=F32,
-                )
-                for m in range(group // SLAB)
-            ],
-            axis=0,
-        )
-        r_send[s] = r_buf[s] - w_buf[s] * landed
-        copy = shift(r_send.at[s], r_buf.at[s + 1], r_send_sem, r_recv_sem.at[s + 1])
-        copy.start()
+        updated = r_buf[s]
+        for halves in two_dots(spread, dense_t):
+            landed = jnp.concatenate([halves[:, :edge], halves[:, edge:]], axis=0)
+            updated = updated - w_buf[s] * landed
+        r_send[s] = updated
+        move = shift(r_send.at[s], r_buf.at[s + 1], r_send_sem, r_recv_sem.at[s + 1])
+        move.start()
 
         @pl.when(s < n_feat - 1)
         def _():
             set_hessian(s + 1)
             set_dense(s + 1, prefix_t, dense_t)
 
-        copy.wait_recv()
+        @pl.when(s == n_feat - 1)
+        def _():
+            set_block(s)
+            pltpu.make_async_copy(beta_v, beta_out, load_sem.at[1]).start()
+
+        move.wait_recv()
         return carry
 
     lax.fori_loop(0, n_feat, section, 0)
 
-    set_block(n_feat - 1)
-    res_out[...] = r_buf[n_feat]
-
-    pltpu.make_async_copy(fifteen, fifteen, m_send_sem).wait()
+    res_copy = pltpu.make_async_copy(r_buf.at[n_feat], res_out, load_sem.at[0])
+    res_copy.start()
+
+    pltpu.make_async_copy(x_recv, x_recv, x_send_sem).wait()
+    pltpu.make_async_copy(m_others, m_others, m_send_sem).wait()
     sent = g_recv.at[:, pl.ds(0, n_samp - 1)]
     pltpu.make_async_copy(sent, sent, g_send_sem).wait()
     sent_r = r_buf.at[pl.ds(0, n_feat)]
     pltpu.make_async_copy(sent_r, sent_r, r_send_sem).wait()
     sent_w = w_buf.at[pl.ds(0, n_feat - 1)]
     pltpu.make_async_copy(sent_w, sent_w, w_send_sem).wait()
+    pltpu.make_async_copy(beta_v, beta_out, load_sem.at[1]).wait()
+    res_copy.wait()
+
+
+def hand_over(beta_ref, res_ref, beta_out, res_out, beta_v, res_v, sems):
+    into = [
+        pltpu.make_async_copy(beta_ref, beta_v, sems.at[0]),
+        pltpu.make_async_copy(res_ref, res_v, sems.at[1]),
+    ]
+    out = [
+        pltpu.make_async_copy(beta_v, beta_out, sems.at[2]),
+        pltpu.make_async_copy(res_v, res_out, sems.at[3]),
+    ]
+    for copy in into:
+        copy.start()
+    for first, second in zip(into, out):
+        first.wait()
+        second.start()
+    for copy in out:
+        copy.wait()
 
 
 def per_device(n_samp, n_feat, labels, beta, tile_rows, tile_cols, tile_values, block_order, hess_inv):
@@ -348,9 +407,10 @@
             jax.ShapeDtypeStruct((group, edge), F32),
         ),
         in_specs=[vmem, vmem, smem, smem, anywhere, anywhere, anywhere, anywhere],
-        out_specs=(vmem, vmem),
+        out_specs=(anywhere, anywhere),
         scratch_shapes=[
             pltpu.VMEM((group, edge), jnp.int32),
+            pltpu.VMEM((feat_blocks, edge), F32),
             pltpu.VMEM((n_tiles, edge, edge), BF16),
             pltpu.VMEM((n_feat, edge, edge), F32),
             pltpu.VMEM((3 * edge, edge), BF16),
@@ -359,11 +419,13 @@
             pltpu.SMEM((1, row_blocks + 2 * edge), jnp.int32),
             pltpu.VMEM((n_tiles + 1, edge, edge), F32),
             pltpu.VMEM((n_tiles + 1, edge, edge), F32),
-            pltpu.VMEM((group, edge, edge), BF16),
-            pltpu.VMEM((group, edge, edge), BF16),
+            pltpu.VMEM((SLAB * edge, group // SLAB * edge), BF16),
+            pltpu.VMEM((SLAB * edge, group // SLAB * edge), BF16),
             pltpu.VMEM((n_feat, 1, edge), F32),
             pltpu.VMEM((n_feat, group, edge), F32),
-            pltpu.VMEM((n_feat, group, edge), F32),
+            pltpu.VMEM((n_feat // 2, group, edge), F32),
+            pltpu.VMEM((n_feat // 2, group, edge), F32),
+            pltpu.VMEM((n_feat // 2, group, edge), F32),
             pltpu.VMEM((n_feat, 1, edge), F32),
             pltpu.VMEM((n_feat, n_samp, 1, edge), F32),
             pltpu.VMEM((n_feat, group, edge), F32),
@@ -372,6 +434,8 @@
             dma((4,)),
             dma(()),
             dma(()),
+            dma((n_feat // 2,)),
+            dma(()),
             dma(()),
             dma(()),
             dma((n_feat,)),
@@ -380,7 +444,9 @@
             dma(()),
             dma((n_feat,)),
         ],
-        compiler_params=pltpu.CompilerParams(collective_id=0, has_side_effects=True),
+        compiler_params=pltpu.CompilerParams(
+            collective_id=0, has_side_effects=True
+        ),
     )(
         tile_rows.reshape(1, n_tiles),
         tile_cols.reshape(1, n_tiles),
@@ -391,6 +457,20 @@
         tile_values.reshape(n_tiles, edge, edge),
         hess_inv.reshape(n_feat, edge, edge),
     )
+    beta_new, residual = pl.pallas_call(
+        hand_over,
+        out_shape=(
+            jax.ShapeDtypeStruct((feat_blocks, edge), F32),
+            jax.ShapeDtypeStruct((group, edge), F32),
+        ),
+        in_specs=[anywhere, anywhere],
+        out_specs=(anywhere, anywhere),
+        scratch_shapes=[
+            pltpu.VMEM((feat_blocks, edge), F32),
+            pltpu.VMEM((group, edge), F32),
+            dma((4,)),
+        ],
+    )(beta_new, residual)
     return beta_new.reshape(-1), residual.reshape(-1)
 
 

time: 180 us -> 178 us (0.989)
  local copies, waits for them, and re-layouts: 2.99 us -> 0 us
    unnamed x2 -> x0, local copies, waits for them, and re-layouts: 2.99 us -> none
where the time goes in v3:
time: 178 us; the launch traced here: 177 us
  Pallas kernels  177 us (99%)
    pallas_call x1, Pallas kernels, per_device(): pl.pallas_call(functools.partial(window_kernel, n_samp, n_feat, n_tiles),...  175 us

profile of v3, /device:TPU:1, one launch (start us, length us, event | category | flops | bytes accessed | tf_op | source)
XLA Modules:
  0.0 177.4 jit_solution(7185779871033610072)
XLA Ops:
  0.6 175.1 %shard_map.86 = (f32[512,128]{1,0:T(8,128)}, f32[32,128]{1,0:T(8,128)}) custom-call(s32[1,64]{1,0:T(1,128)} %bitcast.14, s32[1,64]{1,0:T(1,128)} %bitcast.12, s32[1,64]{1,0:T(1,128)} %bitcast.13, s32[1,16]{1,0:T(1,128)} %order_smem.1, s32[512,128]{1,0:T(8,128)} %bitcast.10, f32[512,128]{1,0:T(8,128)} %bitcast.11, bf16[64,128,128]{2,1,0:T(8,128)(2,1)} %bitcast.8, ...), custom_call_target="tpu_custom_call" | custom-call | tf_op jit(solution)/shard_map/pallas_call | solution.py:403
  175.7 1.7 shard_map.87
